TPU v7x, 512 devices: a whole 4x8x8 slice. The times are simulated.
512 devices in a mesh: board: 8 (over y), sub: 64 (over z, x, core).
Axes of the slice: x: 4, y: 8, z: 8, core: 2. Of those that a mesh axis runs over, the one named last changes fastest.
Arguments:
- rhs: float32 [8, 32, 16384], P('board', None, 'sub')
- schur: float32 [8, 49152, 768], P('board', 'sub'), as said below
- block_list: int32 [8, 384], P('board', 'sub'), may hold values from 0 to 127, as said below
- pad_rows: int32 [8, 4096], P('board', 'sub'), may hold values from 0 to 255, as said below
- pad_cond: float32 [8, 4096], P('board', 'sub'), may hold values from 0.5 to 2
- sink: float32 [8, 16384], P('board', 'sub'), may hold values from 0.2 to 2
- precond: float32 [8, 16384], P('board', 'sub'), may hold values from 0.3 to 1
Outputs:
- solution: float32 [8, 32, 16384], P('board', None, 'sub')
- residual: float32 [8, 32, 16384], P('board', None, 'sub')
Inputs may be any that keep to these rules, and one draw needn't show every extreme that they name: `block_list`: every entry of a subdomain s's list is a block owned by a subdomain at most 3 away from s on the same board; the entries of one list are different and rising, and include all blocks that s owns. `pad_rows`: A subdomain's pad rows are different and rising, and include its first and last owned row. `schur`: each Schur block is symmetric and positive definite.
All inputs are finite; a program needn't handle non-finite values.
Results may differ from a plain program's by a relative error of at most 0.0003.
Values sent between devices are 32-bit elements; how exact they have to be, the bound alone decides.
A program may use at most 64 MiB of HBM per device.

v0:
```python
import jax
import jax.numpy as jnp
from jax import lax
from jax.sharding import PartitionSpec as P

BR = 128
REACH = 3
ITERS = 2


def passed_along(value, axis, steps):
    count = lax.axis_size(axis)
    leading, last = (max(0, -steps), min(count, count - steps))
    return lax.ppermute(value, axis, [(source, source + steps) for source in range(leading, last)])


def from_partner(shard, axis, bit):
    return lax.ppermute(shard, axis, [(i, i ^ 1 << bit) for i in range(lax.axis_size(axis))])


def case_sums(left, right):
    return jnp.sum(left * right, axis=1)


def on_device(rhs, schur, block_list, pad_rows, pad_cond, sink, precond):
    right_side = rhs[0]
    matrix = schur[0]
    block_ids = block_list[0]
    pad_local = pad_rows[0]
    conduct = pad_cond[0]
    sink_rows = sink[0][None, :]
    scaling = precond[0][None, :]
    cases = right_side.shape[0]
    owned_rows = right_side.shape[1]
    blocks_owned = owned_rows // BR
    inner = matrix.shape[0]
    touched = block_ids.shape[0]
    position = lax.axis_index("sub")
    shifted_ids = block_ids - (position - REACH) * blocks_owned
    solution = jnp.zeros_like(right_side)
    residual = right_side
    precon = scaling * residual
    direction = precon
    norm_now = lax.psum(case_sums(residual, precon), ("board", "sub"))
    for iteration in range(ITERS):
        segments = []
        for offset in range(-REACH, REACH + 1):
            if offset == 0:
                segments.append(direction)
            else:
                segments.append(passed_along(direction, "sub", -offset))
        apply_blocks = jnp.concatenate(segments, axis=1).reshape(cases, -1, BR)
        picked = jnp.take(apply_blocks, shifted_ids, axis=1).reshape(cases, inner)
        product = jnp.dot(picked, matrix, precision=lax.Precision.HIGHEST)
        partial_value = (
            jnp.zeros(apply_blocks.shape, jnp.float32)
            .at[:, shifted_ids]
            .add(product.reshape(cases, touched, BR))
        )
        pieces = partial_value.reshape(cases, 2 * REACH + 1, owned_rows)
        result = pieces[:, REACH]
        for offset in range(-REACH, REACH + 1):
            if offset != 0:
                result = result + passed_along(pieces[:, REACH + offset], "sub", offset)
        pad_values = jnp.take(direction, pad_local, axis=1)
        other_values, other_cond = from_partner((pad_values, conduct), "board", 0)
        mean_cond = 0.5 * (conduct + other_cond)
        result = result.at[:, pad_local].add(mean_cond[None, :] * (pad_values - other_values))
        image = result + sink_rows * direction
        final = iteration == ITERS - 1
        curve = lax.psum(case_sums(direction, image), ("board", "sub"))
        alpha = norm_now / curve
        solution = solution + alpha[:, None] * direction
        residual = residual - alpha[:, None] * image
        if not final:
            precon = scaling * residual
            fresh = lax.psum(case_sums(residual, precon), ("board", "sub"))
            direction = precon + (fresh / norm_now)[:, None] * direction
            norm_now = fresh
    return (solution[None], residual[None])


def solution(mesh):
    in_specs = (
        P("board", None, "sub"),
        P("board", "sub", None),
        P("board", "sub"),
        P("board", "sub"),
        P("board", "sub"),
        P("board", "sub"),
        P("board", "sub"),
    )
    out_specs = (P("board", None, "sub"), P("board", None, "sub"))
    return jax.shard_map(
        on_device, mesh=mesh, in_specs=in_specs, out_specs=out_specs, check_vma=False
    )
```

profile of v0, /device:TPU:1, one launch (start us, length us, event | category | flops | bytes accessed | tf_op | source)
XLA Modules:
  0.0 425.5 jit_solution(17108180576712757444)
XLA Ops:
  0.6 0.9 copy.94
  1.5 0.8 bitcast_multiply_fusion.1
  2.3 6.0 %collective-permute-start = (f32[32,256]{0,1:T(8,128)S(1)}, f32[32,256]{0,1:T(8,128)S(1)}, u32[]{:S(2)}, u32[]{:S(2)}) collective-permute-start(f32[32,256]{0,1:T(8,128)S(1)} %bitcast_multiply_fusion.1), channel_id=1, source_target_pairs={{0,3},{1,4},{2,5},{3,6},{4,7},{5,8},{6,9},{7,10},{8,11},{9,12},{10... | collective-permute-start | bytes 98312 | tf_op jit(solution)/shard_map/ppermute | solution.py:14
  8.3 2.2 collective-permute-start.1
  10.5 2.2 collective-permute-start.2
  12.7 2.2 collective-permute-start.3
  15.0 1.3 collective-permute-start.4
  17.6 0.7 compare_and_fusion.1
  18.9 0.7 select_bitcast_fusion.3
  19.6 1.2 fusion.26
  20.8 2.0 copy.104
  22.9 1.3 collective-permute-start.5
  24.2 0.7 copy.95
  24.9 0.8 constant_dynamic-update-slice_fusion.6
  25.6 3.1 collective-permute-start.12
  28.7 0.7 copy.96
  29.4 0.8 constant_dynamic-update-slice_fusion.5
  30.5 1.3 collective-permute-done.5
  32.7 2.2 convolution_bitcast_fusion.1
  34.9 0.7 broadcast.77.clone
  35.6 2.1 scatter_fusion
  37.7 1.2 copy.125
  39.0 4.0 collective-permute-start.10
  43.6 7.4 %collective-permute-start.11 = (f32[32,256]{0,1:T(8,128)S(1)}, f32[32,256]{0,1:T(8,128)S(1)}, u32[]{:S(2)}, u32[]{:S(2)}) collective-permute-start(f32[32,256]{0,1:T(8,128)S(1)} %get-tuple-element.31), channel_id=1, source_target_pairs={{0,3},{1,4},{2,5},{3,6},{4,7},{5,8},{6,9},{7,10},{8,11},{9,12},{10... | collective-permute-start | bytes 98312 | tf_op jit(solution)/shard_map/ppermute | solution.py:14
  51.0 1.3 collective-permute-start.6
  52.3 1.3 collective-permute-start.7
  53.6 1.9 collective-permute-start.8
  55.6 3.6 collective-permute-start.9
  59.2 1.2 add_multiply_fusion
  60.4 3.2 collective-permute-start.13
  63.7 0.8 fusion.14
  64.5 0.9 collective-permute-done.13
  65.4 1.3 scatter_custom_fusion.1
  66.8 108.5 %all-reduce = (f32[32]{0:T(128)S(1)}, f32[32]{0:T(128)S(1)}) all-reduce(f32[32]{0:T(128)S(1)} %get-tuple-element.17, f32[32]{0:T(128)S(1)} %get-tuple-element.16), channel_id=1, replica_groups=mesh['board'=8,'sub'=64] {'board','sub'}, use_global_device_ids=true, to_apply=%region_1.0 | all-reduce | flops 64 | bytes 512 | tf_op jit(solution)/shard_map/psum | solution.py:44
  175.5 94.4 %psum.30 = f32[32]{0:T(128)S(1)} all-reduce(f32[32]{0:T(128)S(1)} %get-tuple-element.20), channel_id=1, replica_groups=mesh['board'=8,'sub'=64] {'board','sub'}, use_global_device_ids=true, to_apply=%region_7.10 | all-reduce | flops 32 | bytes 256 | tf_op jit(solution)/shard_map/psum | solution.py:77
  270.5 3.4 collective-permute-start.14
  274.0 4.0 collective-permute-start.15
  277.9 1.9 collective-permute-start.16
  279.9 2.4 collective-permute-start.17
  282.3 1.3 collective-permute-start.18
  283.7 1.3 collective-permute-start.19
  285.0 0.7 copy.113
  285.6 0.8 constant_dynamic-update-slice_fusion.13
  286.4 1.6 copy.114
  288.0 0.8 constant_dynamic-update-slice_fusion.12
  288.8 0.7 copy.115
  289.5 0.8 constant_dynamic-update-slice_fusion.11
  290.4 1.7 collective-permute-done.19
  292.8 0.8 select_bitcast_fusion
  293.7 2.2 convolution_bitcast_fusion
  295.9 0.8 scatter_fusion.1
  297.1 1.3 collective-permute-start.20
  299.0 1.3 collective-permute-start.21
  300.3 1.9 collective-permute-start.22
  302.2 3.6 collective-permute-start.23
  305.9 5.5 %collective-permute-start.24 = (f32[32,256]{0,1:T(8,128)S(1)}, f32[32,256]{0,1:T(8,128)S(1)}, u32[]{:S(2)}, u32[]{:S(2)}) collective-permute-start(f32[32,256]{0,1:T(8,128)S(1)} %get-tuple-element.26), channel_id=1, source_target_pairs={{0,2},{1,3},{2,4},{3,5},{4,6},{5,7},{6,8},{7,9},{8,10},{9,11},{10,... | collective-permute-start | bytes 98312 | tf_op jit(solution)/shard_map/ppermute | solution.py:14
  311.4 5.2 %collective-permute-start.25 = (f32[32,256]{0,1:T(8,128)S(1)}, f32[32,256]{0,1:T(8,128)S(1)}, u32[]{:S(2)}, u32[]{:S(2)}) collective-permute-start(f32[32,256]{0,1:T(8,128)S(1)} %get-tuple-element.25), channel_id=1, source_target_pairs={{0,3},{1,4},{2,5},{3,6},{4,7},{5,8},{6,9},{7,10},{8,11},{9,12},{10... | collective-permute-start | bytes 98312 | tf_op jit(solution)/shard_map/ppermute | solution.py:14
  316.7 1.9 collective-permute-start.26
  318.6 0.8 collective-permute-done.25
  319.6 2.1 collective-permute-done.26
  321.7 1.2 scatter_custom_fusion.3
  322.9 101.1 %psum.31 = f32[32]{0:T(128)S(1)} all-reduce(f32[32]{0:T(128)S(1)} %multiply_reduce_fusion), channel_id=1, replica_groups=mesh['board'=8,'sub'=64] {'board','sub'}, use_global_device_ids=true, to_apply=%region_11.14 | all-reduce | flops 32 | bytes 256 | tf_op jit(solution)/shard_map/psum | solution.py:71
  424.2 0.7 copy.123
  424.8 0.7 copy.124
  (95 shorter events, 6.9 us)
Async XLA Ops:
  2.3 20.6 %collective-permute-start = (f32[32,256]{0,1:T(8,128)S(1)}, f32[32,256]{0,1:T(8,128)S(1)}, u32[]{:S(2)}, u32[]{:S(2)}) collective-permute-start(f32[32,256]{0,1:T(8,128)S(1)} %bitcast_multiply_fusion.1), channel_id=1, source_target_pairs={{0,3},{1,4},{2,5},{3,6},{4,7},{5,8},{6,9},{7,10},{8,11},{9,12},{10... | collective-permute-start | bytes 98312 | tf_op jit(solution)/shard_map/ppermute | solution.py:14
  8.3 17.3 %collective-permute-start.1 = (f32[32,256]{0,1:T(8,128)S(1)}, f32[32,256]{0,1:T(8,128)S(1)}, u32[]{:S(2)}, u32[]{:S(2)}) collective-permute-start(f32[32,256]{0,1:T(8,128)S(1)} %bitcast_multiply_fusion.1), channel_id=1, source_target_pairs={{0,2},{1,3},{2,4},{3,5},{4,6},{5,7},{6,8},{7,9},{8,10},{9,11},{10,... | collective-permute-start | bytes 98312 | tf_op jit(solution)/shard_map/ppermute | solution.py:14
  10.5 19.6 %collective-permute-start.2 = (f32[32,256]{0,1:T(8,128)S(1)}, f32[32,256]{0,1:T(8,128)S(1)}, u32[]{:S(2)}, u32[]{:S(2)}) collective-permute-start(f32[32,256]{0,1:T(8,128)S(1)} %bitcast_multiply_fusion.1), channel_id=1, source_target_pairs={{0,1},{1,2},{2,3},{3,4},{4,5},{5,6},{6,7},{7,8},{8,9},{9,10},{10,1... | collective-permute-start | bytes 98312 | tf_op jit(solution)/shard_map/ppermute | solution.py:14
  12.7 17.6 %collective-permute-start.3 = (f32[32,256]{0,1:T(8,128)S(1)}, f32[32,256]{0,1:T(8,128)S(1)}, u32[]{:S(2)}, u32[]{:S(2)}) collective-permute-start(f32[32,256]{0,1:T(8,128)S(1)} %bitcast_multiply_fusion.1), channel_id=1, source_target_pairs={{1,0},{2,1},{3,2},{4,3},{5,4},{6,5},{7,6},{8,7},{9,8},{10,9},{11,1... | collective-permute-start | bytes 98312 | tf_op jit(solution)/shard_map/ppermute | solution.py:14
  15.0 15.4 %collective-permute-start.4 = (f32[32,256]{0,1:T(8,128)S(1)}, f32[32,256]{0,1:T(8,128)S(1)}, u32[]{:S(2)}, u32[]{:S(2)}) collective-permute-start(f32[32,256]{0,1:T(8,128)S(1)} %bitcast_multiply_fusion.1), channel_id=1, source_target_pairs={{2,0},{3,1},{4,2},{5,3},{6,4},{7,5},{8,6},{9,7},{10,8},{11,9},{12,... | collective-permute-start | bytes 98312 | tf_op jit(solution)/shard_map/ppermute | solution.py:14
  18.3 14.2 %copy-start.2 = (pred[6]{0:T(512)(128)(4,1)}, pred[6]{0:T(512)(128)(4,1)S(1)}, u32[]{:S(2)}) copy-start(pred[6]{0:T(512)(128)(4,1)S(1)} %get-tuple-element.22) | copy-start | bytes 22
  18.9 1.9 copy-start
  22.9 8.9 %collective-permute-start.5 = (f32[32,256]{0,1:T(8,128)S(1)}, f32[32,256]{0,1:T(8,128)S(1)}, u32[]{:S(2)}, u32[]{:S(2)}) collective-permute-start(f32[32,256]{0,1:T(8,128)S(1)} %bitcast_multiply_fusion.1), channel_id=1, source_target_pairs={{3,0},{4,1},{5,2},{6,3},{7,4},{8,5},{9,6},{10,7},{11,8},{12,9},{13... | collective-permute-start | bytes 98312 | tf_op jit(solution)/shard_map/ppermute | solution.py:14
  25.6 28.0 %collective-permute-start.12 = (f32[64]{0:T(128)}, f32[64]{0:T(128)}, u32[]{:S(2)}, u32[]{:S(2)}) collective-permute-start(f32[64]{0:T(128)} %bitcast.155), channel_id=1, source_target_pairs={{0,64},{64,0},{128,192},{192,128},{256,320},{320,256},{384,448},{4... | collective-permute-start | bytes 776 | tf_op jit(solution)/shard_map/ppermute | solution.py:18
  30.4 5.3 %copy-start.4 = (s32[6]{0:T(128)S(1)}, s32[6]{0:T(128)}, u32[]{:S(2)}) copy-start(s32[6]{0:T(128)} %fusion.26) | copy-start | bytes 76
  32.7 10.3 %copy-start.9 = (s32[1,64]{1,0:T(1,128)S(1)}, s32[1,64]{1,0:T(1,128)}, u32[]{:S(2)}) copy-start(s32[1,64]{1,0:T(1,128)} %param.14) | copy-start | bytes 772
  32.7 26.6 %copy-start.10 = (f32[1,64]{1,0:T(1,128)S(1)}, f32[1,64]{1,0:T(1,128)}, u32[]{:S(2)}) copy-start(f32[1,64]{1,0:T(1,128)} %param.15) | copy-start | bytes 772
  32.7 31.0 %copy-start.1 = (f32[1,256]{1,0:T(1,128)S(1)}, f32[1,256]{1,0:T(1,128)}, u32[]{:S(2)}) copy-start(f32[1,256]{1,0:T(1,128)} %param.17) | copy-start | bytes 3076
  39.0 16.6 %collective-permute-start.10 = (f32[32,256]{0,1:T(8,128)S(1)}, f32[32,256]{0,1:T(8,128)S(1)}, u32[]{:S(2)}, u32[]{:S(2)}) collective-permute-start(f32[32,256]{0,1:T(8,128)S(1)} %get-tuple-element.32), channel_id=1, source_target_pairs={{0,2},{1,3},{2,4},{3,5},{4,6},{5,7},{6,8},{7,9},{8,10},{9,11},{10,... | collective-permute-start | bytes 98312 | tf_op jit(solution)/shard_map/ppermute | solution.py:14
  43.6 16.9 %collective-permute-start.11 = (f32[32,256]{0,1:T(8,128)S(1)}, f32[32,256]{0,1:T(8,128)S(1)}, u32[]{:S(2)}, u32[]{:S(2)}) collective-permute-start(f32[32,256]{0,1:T(8,128)S(1)} %get-tuple-element.31), channel_id=1, source_target_pairs={{0,3},{1,4},{2,5},{3,6},{4,7},{5,8},{6,9},{7,10},{8,11},{9,12},{10... | collective-permute-start | bytes 98312 | tf_op jit(solution)/shard_map/ppermute | solution.py:14
  51.0 12.6 %collective-permute-start.6 = (f32[32,256]{0,1:T(8,128)S(1)}, f32[32,256]{0,1:T(8,128)S(1)}, u32[]{:S(2)}, u32[]{:S(2)}) collective-permute-start(f32[32,256]{0,1:T(8,128)S(1)} %get-tuple-element.30), channel_id=1, source_target_pairs={{3,0},{4,1},{5,2},{6,3},{7,4},{8,5},{9,6},{10,7},{11,8},{12,9},{13... | collective-permute-start | bytes 98312 | tf_op jit(solution)/shard_map/ppermute | solution.py:14
  52.3 11.3 %collective-permute-start.7 = (f32[32,256]{0,1:T(8,128)S(1)}, f32[32,256]{0,1:T(8,128)S(1)}, u32[]{:S(2)}, u32[]{:S(2)}) collective-permute-start(f32[32,256]{0,1:T(8,128)S(1)} %get-tuple-element.35), channel_id=1, source_target_pairs={{2,0},{3,1},{4,2},{5,3},{6,4},{7,5},{8,6},{9,7},{10,8},{11,9},{12,... | collective-permute-start | bytes 98312 | tf_op jit(solution)/shard_map/ppermute | solution.py:14
  53.6 10.0 %collective-permute-start.8 = (f32[32,256]{0,1:T(8,128)S(1)}, f32[32,256]{0,1:T(8,128)S(1)}, u32[]{:S(2)}, u32[]{:S(2)}) collective-permute-start(f32[32,256]{0,1:T(8,128)S(1)} %get-tuple-element.34), channel_id=1, source_target_pairs={{1,0},{2,1},{3,2},{4,3},{5,4},{6,5},{7,6},{8,7},{9,8},{10,9},{11,1... | collective-permute-start | bytes 98312 | tf_op jit(solution)/shard_map/ppermute | solution.py:14
  55.6 8.1 %collective-permute-start.9 = (f32[32,256]{0,1:T(8,128)S(1)}, f32[32,256]{0,1:T(8,128)S(1)}, u32[]{:S(2)}, u32[]{:S(2)}) collective-permute-start(f32[32,256]{0,1:T(8,128)S(1)} %get-tuple-element.33), channel_id=1, source_target_pairs={{0,1},{1,2},{2,3},{3,4},{4,5},{5,6},{6,7},{7,8},{8,9},{9,10},{10,1... | collective-permute-start | bytes 98312 | tf_op jit(solution)/shard_map/ppermute | solution.py:14
  60.4 5.0 %collective-permute-start.13 = (f32[32,64]{0,1:T(8,128)}, f32[32,64]{0,1:T(8,128)}, u32[]{:S(2)}, u32[]{:S(2)}) collective-permute-start(f32[32,64]{0,1:T(8,128)} %select_bitcast_fusion.3), channel_id=1, source_target_pairs={{0,64},{64,0},{128,192},{192,128},{256,320},{320,256},{384,448},{4... | collective-permute-start | bytes 24584 | tf_op jit(solution)/shard_map/ppermute | solution.py:18
  175.4 94.6 %copy-start.7 = (f32[32]{0:T(128)}, f32[32]{0:T(128)S(1)}, u32[]{:S(2)}) copy-start(f32[32]{0:T(128)S(1)} %div.9) | copy-start | bytes 388
  269.9 0.5 copy-start.11
  270.5 13.1 %collective-permute-start.14 = (f32[32,256]{0,1:T(8,128)S(1)}, f32[32,256]{0,1:T(8,128)S(1)}, u32[]{:S(2)}, u32[]{:S(2)}) collective-permute-start(f32[32,256]{0,1:T(8,128)S(1)} %multiply_add_fusion), channel_id=1, source_target_pairs={{0,3},{1,4},{2,5},{3,6},{4,7},{5,8},{6,9},{7,10},{8,11},{9,12},{10... | collective-permute-start | bytes 98312 | tf_op jit(solution)/shard_map/ppermute | solution.py:14
  274.0 12.4 %collective-permute-start.15 = (f32[32,256]{0,1:T(8,128)S(1)}, f32[32,256]{0,1:T(8,128)}, u32[]{:S(2)}, u32[]{:S(2)}) collective-permute-start(f32[32,256]{0,1:T(8,128)S(1)} %multiply_add_fusion), channel_id=1, source_target_pairs={{0,2},{1,3},{2,4},{3,5},{4,6},{5,7},{6,8},{7,9},{8,10},{9,11},{10,... | collective-permute-start | bytes 98312 | tf_op jit(solution)/shard_map/ppermute | solution.py:14
  277.9 10.8 %collective-permute-start.16 = (f32[32,256]{0,1:T(8,128)S(1)}, f32[32,256]{0,1:T(8,128)S(1)}, u32[]{:S(2)}, u32[]{:S(2)}) collective-permute-start(f32[32,256]{0,1:T(8,128)S(1)} %multiply_add_fusion), channel_id=1, source_target_pairs={{0,1},{1,2},{2,3},{3,4},{4,5},{5,6},{6,7},{7,8},{8,9},{9,10},{10,1... | collective-permute-start | bytes 98312 | tf_op jit(solution)/shard_map/ppermute | solution.py:14
  279.9 10.3 %collective-permute-start.17 = (f32[32,256]{0,1:T(8,128)S(1)}, f32[32,256]{0,1:T(8,128)S(1)}, u32[]{:S(2)}, u32[]{:S(2)}) collective-permute-start(f32[32,256]{0,1:T(8,128)S(1)} %multiply_add_fusion), channel_id=1, source_target_pairs={{1,0},{2,1},{3,2},{4,3},{5,4},{6,5},{7,6},{8,7},{9,8},{10,9},{11,1... | collective-permute-start | bytes 98312 | tf_op jit(solution)/shard_map/ppermute | solution.py:14
  282.3 8.0 %collective-permute-start.18 = (f32[32,256]{0,1:T(8,128)S(1)}, f32[32,256]{0,1:T(8,128)S(1)}, u32[]{:S(2)}, u32[]{:S(2)}) collective-permute-start(f32[32,256]{0,1:T(8,128)S(1)} %multiply_add_fusion), channel_id=1, source_target_pairs={{2,0},{3,1},{4,2},{5,3},{6,4},{7,5},{8,6},{9,7},{10,8},{11,9},{12,... | collective-permute-start | bytes 98312 | tf_op jit(solution)/shard_map/ppermute | solution.py:14
  283.7 8.5 %collective-permute-start.19 = (f32[32,256]{0,1:T(8,128)S(1)}, f32[32,256]{0,1:T(8,128)S(1)}, u32[]{:S(2)}, u32[]{:S(2)}) collective-permute-start(f32[32,256]{0,1:T(8,128)S(1)} %multiply_add_fusion), channel_id=1, source_target_pairs={{3,0},{4,1},{5,2},{6,3},{7,4},{8,5},{9,6},{10,7},{11,8},{12,9},{13... | collective-permute-start | bytes 98312 | tf_op jit(solution)/shard_map/ppermute | solution.py:14
  290.3 5.6 %copy-start.5 = (s32[6]{0:T(128)S(1)}, s32[6]{0:T(128)}, u32[]{:S(2)}) copy-start(s32[6]{0:T(128)} %fusion.26) | copy-start | bytes 76
  295.9 23.6 %copy-start.3 = (f32[1,256]{1,0:T(1,128)S(1)}, f32[1,256]{1,0:T(1,128)}, u32[]{:S(2)}) copy-start(f32[1,256]{1,0:T(1,128)} %param.16) | copy-start | bytes 3076
  295.9 25.8 %copy-start.6 = (f32[64]{0:T(128)S(1)}, f32[64]{0:T(128)}, u32[]{:S(2)}) copy-start(f32[64]{0:T(128)} %add_multiply_fusion) | copy-start | bytes 772
  296.7 127.3 %copy-start.12 = (f32[32]{0:T(128)S(1)}, f32[32]{0:T(128)}, u32[]{:S(2)}) copy-start(f32[32]{0:T(128)} %copy-done.11) | copy-start | bytes 388
  296.7 127.3 %copy-start.8 = (f32[32]{0:T(128)S(1)}, f32[32]{0:T(128)}, u32[]{:S(2)}) copy-start(f32[32]{0:T(128)} %copy-done.7) | copy-start | bytes 388
  297.1 14.3 %collective-permute-start.20 = (f32[32,256]{0,1:T(8,128)S(1)}, f32[32,256]{0,1:T(8,128)S(1)}, u32[]{:S(2)}, u32[]{:S(2)}) collective-permute-start(f32[32,256]{0,1:T(8,128)S(1)} %get-tuple-element.24), channel_id=1, source_target_pairs={{3,0},{4,1},{5,2},{6,3},{7,4},{8,5},{9,6},{10,7},{11,8},{12,9},{13... | collective-permute-start | bytes 98312 | tf_op jit(solution)/shard_map/ppermute | solution.py:14
  299.0 17.6 %collective-permute-start.21 = (f32[32,256]{0,1:T(8,128)S(1)}, f32[32,256]{0,1:T(8,128)S(1)}, u32[]{:S(2)}, u32[]{:S(2)}) collective-permute-start(f32[32,256]{0,1:T(8,128)S(1)} %get-tuple-element.29), channel_id=1, source_target_pairs={{2,0},{3,1},{4,2},{5,3},{6,4},{7,5},{8,6},{9,7},{10,8},{11,9},{12,... | collective-permute-start | bytes 98312 | tf_op jit(solution)/shard_map/ppermute | solution.py:14
  300.3 18.3 %collective-permute-start.22 = (f32[32,256]{0,1:T(8,128)S(1)}, f32[32,256]{0,1:T(8,128)S(1)}, u32[]{:S(2)}, u32[]{:S(2)}) collective-permute-start(f32[32,256]{0,1:T(8,128)S(1)} %get-tuple-element.28), channel_id=1, source_target_pairs={{1,0},{2,1},{3,2},{4,3},{5,4},{6,5},{7,6},{8,7},{9,8},{10,9},{11,1... | collective-permute-start | bytes 98312 | tf_op jit(solution)/shard_map/ppermute | solution.py:14
  302.2 16.4 %collective-permute-start.23 = (f32[32,256]{0,1:T(8,128)S(1)}, f32[32,256]{0,1:T(8,128)S(1)}, u32[]{:S(2)}, u32[]{:S(2)}) collective-permute-start(f32[32,256]{0,1:T(8,128)S(1)} %get-tuple-element.27), channel_id=1, source_target_pairs={{0,1},{1,2},{2,3},{3,4},{4,5},{5,6},{6,7},{7,8},{8,9},{9,10},{10,1... | collective-permute-start | bytes 98312 | tf_op jit(solution)/shard_map/ppermute | solution.py:14
  305.9 12.7 %collective-permute-start.24 = (f32[32,256]{0,1:T(8,128)S(1)}, f32[32,256]{0,1:T(8,128)S(1)}, u32[]{:S(2)}, u32[]{:S(2)}) collective-permute-start(f32[32,256]{0,1:T(8,128)S(1)} %get-tuple-element.26), channel_id=1, source_target_pairs={{0,2},{1,3},{2,4},{3,5},{4,6},{5,7},{6,8},{7,9},{8,10},{9,11},{10,... | collective-permute-start | bytes 98312 | tf_op jit(solution)/shard_map/ppermute | solution.py:14
  311.4 8.0 %collective-permute-start.25 = (f32[32,256]{0,1:T(8,128)S(1)}, f32[32,256]{0,1:T(8,128)S(1)}, u32[]{:S(2)}, u32[]{:S(2)}) collective-permute-start(f32[32,256]{0,1:T(8,128)S(1)} %get-tuple-element.25), channel_id=1, source_target_pairs={{0,3},{1,4},{2,5},{3,6},{4,7},{5,8},{6,9},{7,10},{8,11},{9,12},{10... | collective-permute-start | bytes 98312 | tf_op jit(solution)/shard_map/ppermute | solution.py:14
  316.7 5.0 %collective-permute-start.26 = (f32[32,64]{0,1:T(8,128)S(1)}, f32[32,64]{0,1:T(8,128)S(1)}, u32[]{:S(2)}, u32[]{:S(2)}) collective-permute-start(f32[32,64]{0,1:T(8,128)S(1)} %select_bitcast_fusion.2), channel_id=1, source_target_pairs={{0,64},{64,0},{128,192},{192,128},{256,320},{320,256},{384,448},{4... | collective-permute-start | bytes 24584 | tf_op jit(solution)/shard_map/ppermute | solution.py:18
where the time goes:
time: 427 us; the launch traced here: 426 us
  blocking collectives  304 us (71%)
  starting transfers between devices  76.1 us (18%)
  local copies, waits for them, and re-layouts  18.5 us (4%)
  other arithmetic  14.1 us (3%)
  waiting for transfers between devices  6.94 us (2%)
  matrix products  4.43 us (1%)
    psum x1, blocking collectives, on_device(): norm_now = lax.psum(case_sums(residual, precon), ('board', 'sub'))  109 us
    psum x1, blocking collectives, on_device(): curve = lax.psum(case_sums(direction, image), ('board', 'sub'))  101 us
    psum x1, blocking collectives, on_device(): fresh = lax.psum(case_sums(residual, precon), ('board', 'sub'))  94.4 us
    ppermute x24, starting transfers between devices, passed_along(): lax.ppermute(value, axis, [(source, source + steps) for source in range(l...  67.9 us
    unnamed x42, local copies, waits for them, and re-layouts  8.71 us
  transfers between devices with their start and end apart: 27, of which 5 were waited for; matrix products, arithmetic and copies ran while one was open for 6% of the time, Pallas kernels for 0%

commit v1 on v0

--- a/solution.py
+++ b/solution.py
@@ -68,7 +68,7 @@
         result = result.at[:, pad_local].add(mean_cond[None, :] * (pad_values - other_values))
         image = result + sink_rows * direction
         final = iteration == ITERS - 1
-        curve = lax.psum(case_sums(direction, image), ("board", "sub"))
+        curve = lax.psum(lax.psum(case_sums(direction, image), "board"), "sub")
         alpha = norm_now / curve
         solution = solution + alpha[:, None] * direction
         residual = residual - alpha[:, None] * image

time: 427 us -> 605 us (1.42)
  blocking collectives: 304 us -> 480 us
    psum x1 -> x4, blocking collectives: 101 us -> 287 us  [on_device(): curve = lax.psum(lax.psum(case_sums(direction, image), 'board'), 'sub')]
    psum x1, blocking collectives: 109 us -> 98.5 us  [on_device(): norm_now = lax.psum(case_sums(residual, precon), ('board', 'sub'))]
  transfers between devices with their start and end apart: 27 -> 27, of which waited for: 5 -> 5; matrix products, arithmetic and copies ran while one was open for 6% -> 4% of each run, Pallas kernels for 0% -> 0%
where the time goes in v1:
time: 605 us; the launch traced here: 601 us
  blocking collectives  480 us (79%)
  starting transfers between devices  75.7 us (13%)
  local copies, waits for them, and re-layouts  18.5 us (3%)
  other arithmetic  14 us (2%)
  waiting for transfers between devices  7.37 us (1%)
    psum x4, blocking collectives, on_device(): curve = lax.psum(lax.psum(case_sums(direction, image), 'board'), 'sub')  287 us
    psum x1, blocking collectives, on_device(): norm_now = lax.psum(case_sums(residual, precon), ('board', 'sub'))  98.5 us
    psum x1, blocking collectives, on_device(): fresh = lax.psum(case_sums(residual, precon), ('board', 'sub'))  94.4 us
    ppermute x24, starting transfers between devices, passed_along(): lax.ppermute(value, axis, [(source, source + steps) for source in range(l...  67.4 us
  transfers between devices with their start and end apart: 27, of which 5 were waited for; matrix products, arithmetic and copies ran while one was open for 4% of the time, Pallas kernels for 0%

profile of v1, /device:TPU:1, one launch (start us, length us, event | category | flops | bytes accessed | tf_op | source)
XLA Modules:
  0.0 601.5 jit_solution(11939809743344124730)
XLA Ops:
  0.6 0.9 copy.94
  1.5 0.8 bitcast_multiply_fusion.1
  2.3 6.0 %collective-permute-start = (f32[32,256]{0,1:T(8,128)S(1)}, f32[32,256]{0,1:T(8,128)S(1)}, u32[]{:S(2)}, u32[]{:S(2)}) collective-permute-start(f32[32,256]{0,1:T(8,128)S(1)} %bitcast_multiply_fusion.1), channel_id=1, source_target_pairs={{0,3},{1,4},{2,5},{3,6},{4,7},{5,8},{6,9},{7,10},{8,11},{9,12},{10... | collective-permute-start | bytes 98312 | tf_op jit(solution)/shard_map/ppermute | solution.py:14
  8.3 2.2 collective-permute-start.1
  10.5 2.2 collective-permute-start.2
  12.7 2.2 collective-permute-start.3
  15.0 1.3 collective-permute-start.4
  18.9 0.7 select_bitcast_fusion.3
  19.6 1.2 fusion.26
  20.8 2.0 copy.104
  22.9 1.3 collective-permute-start.5
  24.2 0.7 copy.95
  24.9 0.8 constant_dynamic-update-slice_fusion.6
  25.7 3.1 collective-permute-start.12
  28.8 0.7 copy.96
  29.5 0.8 constant_dynamic-update-slice_fusion.5
  30.5 1.3 collective-permute-done.5
  32.7 2.2 convolution_bitcast_fusion.1
  35.0 0.7 broadcast.77.clone
  35.7 2.1 scatter_fusion
  37.8 1.2 copy.125
  39.1 4.0 collective-permute-start.10
  43.6 7.4 %collective-permute-start.11 = (f32[32,256]{0,1:T(8,128)S(1)}, f32[32,256]{0,1:T(8,128)S(1)}, u32[]{:S(2)}, u32[]{:S(2)}) collective-permute-start(f32[32,256]{0,1:T(8,128)S(1)} %get-tuple-element.29), channel_id=1, source_target_pairs={{0,3},{1,4},{2,5},{3,6},{4,7},{5,8},{6,9},{7,10},{8,11},{9,12},{10... | collective-permute-start | bytes 98312 | tf_op jit(solution)/shard_map/ppermute | solution.py:14
  51.0 1.3 collective-permute-start.6
  52.3 1.3 collective-permute-start.7
  53.6 1.9 collective-permute-start.8
  55.6 3.6 collective-permute-start.9
  59.2 1.2 add_multiply_fusion
  60.4 3.2 collective-permute-start.13
  63.7 0.8 fusion.14
  64.5 0.9 collective-permute-done.13
  65.4 1.3 scatter_custom_fusion.1
  66.8 13.9 %psum.43 = f32[32]{0:T(128)S(1)} all-reduce(f32[32]{0:T(128)S(1)} %get-tuple-element.16), channel_id=1, replica_groups=mesh['board'=8,'sub'=64] {'board'}, use_global_device_ids=true, to_apply=%region_5.8 | all-reduce | flops 32 | bytes 256 | tf_op jit(solution)/shard_map/psum | solution.py:71
  80.7 134.9 %psum.44 = f32[32]{0:T(128)S(1)} all-reduce(f32[32]{0:T(128)S(1)} %psum.43), channel_id=1, replica_groups=mesh['board'=8,'sub'=64] {'sub'}, use_global_device_ids=true, to_apply=%region_6.9 | all-reduce | flops 32 | bytes 256 | tf_op jit(solution)/shard_map/psum | solution.py:71
  215.6 98.5 %psum.42 = f32[32]{0:T(128)S(1)} all-reduce(f32[32]{0:T(128)S(1)} %get-tuple-element.17), channel_id=1, replica_groups=mesh['board'=8,'sub'=64] {'board','sub'}, use_global_device_ids=true, to_apply=%region_1.0 | all-reduce | flops 32 | bytes 256 | tf_op jit(solution)/shard_map/psum | solution.py:44
  314.2 94.4 %psum.45 = f32[32]{0:T(128)S(1)} all-reduce(f32[32]{0:T(128)S(1)} %get-tuple-element.18), channel_id=1, replica_groups=mesh['board'=8,'sub'=64] {'board','sub'}, use_global_device_ids=true, to_apply=%region_8.11 | all-reduce | flops 32 | bytes 256 | tf_op jit(solution)/shard_map/psum | solution.py:77
  409.3 3.1 collective-permute-start.14
  412.4 3.4 collective-permute-start.15
  415.8 1.9 collective-permute-start.16
  417.8 2.4 collective-permute-start.17
  420.2 1.3 collective-permute-start.18
  421.5 1.3 collective-permute-start.19
  422.8 0.7 copy.113
  423.5 0.8 constant_dynamic-update-slice_fusion.13
  424.3 1.6 copy.114
  425.9 0.8 constant_dynamic-update-slice_fusion.12
  426.6 0.7 copy.115
  427.3 0.8 constant_dynamic-update-slice_fusion.11
  428.3 2.4 collective-permute-done.19
  432.1 2.2 convolution_bitcast_fusion
  434.4 0.8 scatter_fusion.1
  435.6 1.3 collective-permute-start.20
  437.5 1.3 collective-permute-start.21
  438.8 1.9 collective-permute-start.22
  440.7 3.6 collective-permute-start.23
  444.3 5.4 collective-permute-start.24
  449.7 5.7 collective-permute-start.25
  455.5 1.9 collective-permute-start.26
  457.5 0.7 collective-permute-done.25
  458.3 2.0 collective-permute-done.26
  460.3 1.2 scatter_custom_fusion.3
  461.6 10.9 %psum.46 = f32[32]{0:T(128)S(1)} all-reduce(f32[32]{0:T(128)S(1)} %multiply_reduce_fusion), channel_id=1, replica_groups=mesh['board'=8,'sub'=64] {'board'}, use_global_device_ids=true, to_apply=%region_12.15 | all-reduce | flops 32 | bytes 256 | tf_op jit(solution)/shard_map/psum | solution.py:71
  472.5 127.5 %psum.47 = f32[32]{0:T(128)S(1)} all-reduce(f32[32]{0:T(128)S(1)} %psum.46), channel_id=1, replica_groups=mesh['board'=8,'sub'=64] {'sub'}, use_global_device_ids=true, to_apply=%region_13.16 | all-reduce | flops 32 | bytes 256 | tf_op jit(solution)/shard_map/psum | solution.py:71
  600.1 0.7 copy.123
  (98 shorter events, 8.9 us)
Async XLA Ops:
  2.3 20.6 %collective-permute-start = (f32[32,256]{0,1:T(8,128)S(1)}, f32[32,256]{0,1:T(8,128)S(1)}, u32[]{:S(2)}, u32[]{:S(2)}) collective-permute-start(f32[32,256]{0,1:T(8,128)S(1)} %bitcast_multiply_fusion.1), channel_id=1, source_target_pairs={{0,3},{1,4},{2,5},{3,6},{4,7},{5,8},{6,9},{7,10},{8,11},{9,12},{10... | collective-permute-start | bytes 98312 | tf_op jit(solution)/shard_map/ppermute | solution.py:14
  8.3 17.3 %collective-permute-start.1 = (f32[32,256]{0,1:T(8,128)S(1)}, f32[32,256]{0,1:T(8,128)S(1)}, u32[]{:S(2)}, u32[]{:S(2)}) collective-permute-start(f32[32,256]{0,1:T(8,128)S(1)} %bitcast_multiply_fusion.1), channel_id=1, source_target_pairs={{0,2},{1,3},{2,4},{3,5},{4,6},{5,7},{6,8},{7,9},{8,10},{9,11},{10,... | collective-permute-start | bytes 98312 | tf_op jit(solution)/shard_map/ppermute | solution.py:14
  10.5 19.7 %collective-permute-start.2 = (f32[32,256]{0,1:T(8,128)S(1)}, f32[32,256]{0,1:T(8,128)S(1)}, u32[]{:S(2)}, u32[]{:S(2)}) collective-permute-start(f32[32,256]{0,1:T(8,128)S(1)} %bitcast_multiply_fusion.1), channel_id=1, source_target_pairs={{0,1},{1,2},{2,3},{3,4},{4,5},{5,6},{6,7},{7,8},{8,9},{9,10},{10,1... | collective-permute-start | bytes 98312 | tf_op jit(solution)/shard_map/ppermute | solution.py:14
  12.7 17.6 %collective-permute-start.3 = (f32[32,256]{0,1:T(8,128)S(1)}, f32[32,256]{0,1:T(8,128)S(1)}, u32[]{:S(2)}, u32[]{:S(2)}) collective-permute-start(f32[32,256]{0,1:T(8,128)S(1)} %bitcast_multiply_fusion.1), channel_id=1, source_target_pairs={{1,0},{2,1},{3,2},{4,3},{5,4},{6,5},{7,6},{8,7},{9,8},{10,9},{11,1... | collective-permute-start | bytes 98312 | tf_op jit(solution)/shard_map/ppermute | solution.py:14
  15.0 15.5 %collective-permute-start.4 = (f32[32,256]{0,1:T(8,128)S(1)}, f32[32,256]{0,1:T(8,128)S(1)}, u32[]{:S(2)}, u32[]{:S(2)}) collective-permute-start(f32[32,256]{0,1:T(8,128)S(1)} %bitcast_multiply_fusion.1), channel_id=1, source_target_pairs={{2,0},{3,1},{4,2},{5,3},{6,4},{7,5},{8,6},{9,7},{10,8},{11,9},{12,... | collective-permute-start | bytes 98312 | tf_op jit(solution)/shard_map/ppermute | solution.py:14
  18.3 14.3 %copy-start.2 = (pred[6]{0:T(512)(128)(4,1)}, pred[6]{0:T(512)(128)(4,1)S(1)}, u32[]{:S(2)}) copy-start(pred[6]{0:T(512)(128)(4,1)S(1)} %get-tuple-element.20) | copy-start | bytes 22
  18.9 1.9 copy-start
  22.9 8.9 %collective-permute-start.5 = (f32[32,256]{0,1:T(8,128)S(1)}, f32[32,256]{0,1:T(8,128)S(1)}, u32[]{:S(2)}, u32[]{:S(2)}) collective-permute-start(f32[32,256]{0,1:T(8,128)S(1)} %bitcast_multiply_fusion.1), channel_id=1, source_target_pairs={{3,0},{4,1},{5,2},{6,3},{7,4},{8,5},{9,6},{10,7},{11,8},{12,9},{13... | collective-permute-start | bytes 98312 | tf_op jit(solution)/shard_map/ppermute | solution.py:14
  25.7 28.0 %collective-permute-start.12 = (f32[64]{0:T(128)}, f32[64]{0:T(128)}, u32[]{:S(2)}, u32[]{:S(2)}) collective-permute-start(f32[64]{0:T(128)} %bitcast.155), channel_id=1, source_target_pairs={{0,64},{64,0},{128,192},{192,128},{256,320},{320,256},{384,448},{4... | collective-permute-start | bytes 776 | tf_op jit(solution)/shard_map/ppermute | solution.py:18
  30.4 5.3 copy-start.4
  32.7 10.3 %copy-start.9 = (s32[1,64]{1,0:T(1,128)S(1)}, s32[1,64]{1,0:T(1,128)}, u32[]{:S(2)}) copy-start(s32[1,64]{1,0:T(1,128)} %param.14) | copy-start | bytes 772
  32.7 26.5 %copy-start.10 = (f32[1,64]{1,0:T(1,128)S(1)}, f32[1,64]{1,0:T(1,128)}, u32[]{:S(2)}) copy-start(f32[1,64]{1,0:T(1,128)} %param.15) | copy-start | bytes 772
  32.7 31.0 %copy-start.1 = (f32[1,256]{1,0:T(1,128)S(1)}, f32[1,256]{1,0:T(1,128)}, u32[]{:S(2)}) copy-start(f32[1,256]{1,0:T(1,128)} %param.17) | copy-start | bytes 3076
  39.1 16.5 %collective-permute-start.10 = (f32[32,256]{0,1:T(8,128)S(1)}, f32[32,256]{0,1:T(8,128)S(1)}, u32[]{:S(2)}, u32[]{:S(2)}) collective-permute-start(f32[32,256]{0,1:T(8,128)S(1)} %get-tuple-element.30), channel_id=1, source_target_pairs={{0,2},{1,3},{2,4},{3,5},{4,6},{5,7},{6,8},{7,9},{8,10},{9,11},{10,... | collective-permute-start | bytes 98312 | tf_op jit(solution)/shard_map/ppermute | solution.py:14
  43.6 16.9 %collective-permute-start.11 = (f32[32,256]{0,1:T(8,128)S(1)}, f32[32,256]{0,1:T(8,128)S(1)}, u32[]{:S(2)}, u32[]{:S(2)}) collective-permute-start(f32[32,256]{0,1:T(8,128)S(1)} %get-tuple-element.29), channel_id=1, source_target_pairs={{0,3},{1,4},{2,5},{3,6},{4,7},{5,8},{6,9},{7,10},{8,11},{9,12},{10... | collective-permute-start | bytes 98312 | tf_op jit(solution)/shard_map/ppermute | solution.py:14
  51.0 12.6 %collective-permute-start.6 = (f32[32,256]{0,1:T(8,128)S(1)}, f32[32,256]{0,1:T(8,128)S(1)}, u32[]{:S(2)}, u32[]{:S(2)}) collective-permute-start(f32[32,256]{0,1:T(8,128)S(1)} %get-tuple-element.28), channel_id=1, source_target_pairs={{3,0},{4,1},{5,2},{6,3},{7,4},{8,5},{9,6},{10,7},{11,8},{12,9},{13... | collective-permute-start | bytes 98312 | tf_op jit(solution)/shard_map/ppermute | solution.py:14
  52.3 11.4 %collective-permute-start.7 = (f32[32,256]{0,1:T(8,128)S(1)}, f32[32,256]{0,1:T(8,128)S(1)}, u32[]{:S(2)}, u32[]{:S(2)}) collective-permute-start(f32[32,256]{0,1:T(8,128)S(1)} %get-tuple-element.33), channel_id=1, source_target_pairs={{2,0},{3,1},{4,2},{5,3},{6,4},{7,5},{8,6},{9,7},{10,8},{11,9},{12,... | collective-permute-start | bytes 98312 | tf_op jit(solution)/shard_map/ppermute | solution.py:14
  53.6 10.1 %collective-permute-start.8 = (f32[32,256]{0,1:T(8,128)S(1)}, f32[32,256]{0,1:T(8,128)S(1)}, u32[]{:S(2)}, u32[]{:S(2)}) collective-permute-start(f32[32,256]{0,1:T(8,128)S(1)} %get-tuple-element.32), channel_id=1, source_target_pairs={{1,0},{2,1},{3,2},{4,3},{5,4},{6,5},{7,6},{8,7},{9,8},{10,9},{11,1... | collective-permute-start | bytes 98312 | tf_op jit(solution)/shard_map/ppermute | solution.py:14
  55.6 8.1 %collective-permute-start.9 = (f32[32,256]{0,1:T(8,128)S(1)}, f32[32,256]{0,1:T(8,128)S(1)}, u32[]{:S(2)}, u32[]{:S(2)}) collective-permute-start(f32[32,256]{0,1:T(8,128)S(1)} %get-tuple-element.31), channel_id=1, source_target_pairs={{0,1},{1,2},{2,3},{3,4},{4,5},{5,6},{6,7},{7,8},{8,9},{9,10},{10,1... | collective-permute-start | bytes 98312 | tf_op jit(solution)/shard_map/ppermute | solution.py:14
  60.4 5.0 collective-permute-start.13
  314.1 94.6 %copy-start.7 = (f32[32]{0:T(128)}, f32[32]{0:T(128)S(1)}, u32[]{:S(2)}) copy-start(f32[32]{0:T(128)S(1)} %div.9) | copy-start | bytes 388
  408.7 0.5 copy-start.11
  409.3 12.2 %collective-permute-start.14 = (f32[32,256]{0,1:T(8,128)S(1)}, f32[32,256]{0,1:T(8,128)S(1)}, u32[]{:S(2)}, u32[]{:S(2)}) collective-permute-start(f32[32,256]{0,1:T(8,128)S(1)} %multiply_add_fusion), channel_id=1, source_target_pairs={{0,3},{1,4},{2,5},{3,6},{4,7},{5,8},{6,9},{7,10},{8,11},{9,12},{10... | collective-permute-start | bytes 98312 | tf_op jit(solution)/shard_map/ppermute | solution.py:14
  412.4 11.9 %collective-permute-start.15 = (f32[32,256]{0,1:T(8,128)S(1)}, f32[32,256]{0,1:T(8,128)}, u32[]{:S(2)}, u32[]{:S(2)}) collective-permute-start(f32[32,256]{0,1:T(8,128)S(1)} %multiply_add_fusion), channel_id=1, source_target_pairs={{0,2},{1,3},{2,4},{3,5},{4,6},{5,7},{6,8},{7,9},{8,10},{9,11},{10,... | collective-permute-start | bytes 98312 | tf_op jit(solution)/shard_map/ppermute | solution.py:14
  415.8 10.8 %collective-permute-start.16 = (f32[32,256]{0,1:T(8,128)S(1)}, f32[32,256]{0,1:T(8,128)S(1)}, u32[]{:S(2)}, u32[]{:S(2)}) collective-permute-start(f32[32,256]{0,1:T(8,128)S(1)} %multiply_add_fusion), channel_id=1, source_target_pairs={{0,1},{1,2},{2,3},{3,4},{4,5},{5,6},{6,7},{7,8},{8,9},{9,10},{10,1... | collective-permute-start | bytes 98312 | tf_op jit(solution)/shard_map/ppermute | solution.py:14
  417.8 10.3 %collective-permute-start.17 = (f32[32,256]{0,1:T(8,128)S(1)}, f32[32,256]{0,1:T(8,128)S(1)}, u32[]{:S(2)}, u32[]{:S(2)}) collective-permute-start(f32[32,256]{0,1:T(8,128)S(1)} %multiply_add_fusion), channel_id=1, source_target_pairs={{1,0},{2,1},{3,2},{4,3},{5,4},{6,5},{7,6},{8,7},{9,8},{10,9},{11,1... | collective-permute-start | bytes 98312 | tf_op jit(solution)/shard_map/ppermute | solution.py:14
  420.2 8.0 %collective-permute-start.18 = (f32[32,256]{0,1:T(8,128)S(1)}, f32[32,256]{0,1:T(8,128)S(1)}, u32[]{:S(2)}, u32[]{:S(2)}) collective-permute-start(f32[32,256]{0,1:T(8,128)S(1)} %multiply_add_fusion), channel_id=1, source_target_pairs={{2,0},{3,1},{4,2},{5,3},{6,4},{7,5},{8,6},{9,7},{10,8},{11,9},{12,... | collective-permute-start | bytes 98312 | tf_op jit(solution)/shard_map/ppermute | solution.py:14
  421.5 9.1 %collective-permute-start.19 = (f32[32,256]{0,1:T(8,128)S(1)}, f32[32,256]{0,1:T(8,128)S(1)}, u32[]{:S(2)}, u32[]{:S(2)}) collective-permute-start(f32[32,256]{0,1:T(8,128)S(1)} %multiply_add_fusion), channel_id=1, source_target_pairs={{3,0},{4,1},{5,2},{6,3},{7,4},{8,5},{9,6},{10,7},{11,8},{12,9},{13... | collective-permute-start | bytes 98312 | tf_op jit(solution)/shard_map/ppermute | solution.py:14
  428.2 6.2 %copy-start.5 = (s32[6]{0:T(128)S(1)}, s32[6]{0:T(128)}, u32[]{:S(2)}) copy-start(s32[6]{0:T(128)} %fusion.26) | copy-start | bytes 76
  434.3 23.9 %copy-start.3 = (f32[1,256]{1,0:T(1,128)S(1)}, f32[1,256]{1,0:T(1,128)}, u32[]{:S(2)}) copy-start(f32[1,256]{1,0:T(1,128)} %param.16) | copy-start | bytes 3076
  434.4 26.0 %copy-start.6 = (f32[64]{0:T(128)S(1)}, f32[64]{0:T(128)}, u32[]{:S(2)}) copy-start(f32[64]{0:T(128)} %add_multiply_fusion) | copy-start | bytes 772
  435.2 164.8 %copy-start.12 = (f32[32]{0:T(128)S(1)}, f32[32]{0:T(128)}, u32[]{:S(2)}) copy-start(f32[32]{0:T(128)} %copy-done.11) | copy-start | bytes 388
  435.2 164.8 %copy-start.8 = (f32[32]{0:T(128)S(1)}, f32[32]{0:T(128)}, u32[]{:S(2)}) copy-start(f32[32]{0:T(128)} %copy-done.7) | copy-start | bytes 388
  435.6 14.2 %collective-permute-start.20 = (f32[32,256]{0,1:T(8,128)S(1)}, f32[32,256]{0,1:T(8,128)S(1)}, u32[]{:S(2)}, u32[]{:S(2)}) collective-permute-start(f32[32,256]{0,1:T(8,128)S(1)} %get-tuple-element.22), channel_id=1, source_target_pairs={{3,0},{4,1},{5,2},{6,3},{7,4},{8,5},{9,6},{10,7},{11,8},{12,9},{13... | collective-permute-start | bytes 98312 | tf_op jit(solution)/shard_map/ppermute | solution.py:14
  437.5 18.1 %collective-permute-start.21 = (f32[32,256]{0,1:T(8,128)S(1)}, f32[32,256]{0,1:T(8,128)S(1)}, u32[]{:S(2)}, u32[]{:S(2)}) collective-permute-start(f32[32,256]{0,1:T(8,128)S(1)} %get-tuple-element.27), channel_id=1, source_target_pairs={{2,0},{3,1},{4,2},{5,3},{6,4},{7,5},{8,6},{9,7},{10,8},{11,9},{12,... | collective-permute-start | bytes 98312 | tf_op jit(solution)/shard_map/ppermute | solution.py:14
  438.8 18.7 %collective-permute-start.22 = (f32[32,256]{0,1:T(8,128)S(1)}, f32[32,256]{0,1:T(8,128)S(1)}, u32[]{:S(2)}, u32[]{:S(2)}) collective-permute-start(f32[32,256]{0,1:T(8,128)S(1)} %get-tuple-element.26), channel_id=1, source_target_pairs={{1,0},{2,1},{3,2},{4,3},{5,4},{6,5},{7,6},{8,7},{9,8},{10,9},{11,1... | collective-permute-start | bytes 98312 | tf_op jit(solution)/shard_map/ppermute | solution.py:14
  440.7 16.8 %collective-permute-start.23 = (f32[32,256]{0,1:T(8,128)S(1)}, f32[32,256]{0,1:T(8,128)S(1)}, u32[]{:S(2)}, u32[]{:S(2)}) collective-permute-start(f32[32,256]{0,1:T(8,128)S(1)} %get-tuple-element.25), channel_id=1, source_target_pairs={{0,1},{1,2},{2,3},{3,4},{4,5},{5,6},{6,7},{7,8},{8,9},{9,10},{10,1... | collective-permute-start | bytes 98312 | tf_op jit(solution)/shard_map/ppermute | solution.py:14
  444.3 13.1 %collective-permute-start.24 = (f32[32,256]{0,1:T(8,128)S(1)}, f32[32,256]{0,1:T(8,128)S(1)}, u32[]{:S(2)}, u32[]{:S(2)}) collective-permute-start(f32[32,256]{0,1:T(8,128)S(1)} %get-tuple-element.24), channel_id=1, source_target_pairs={{0,2},{1,3},{2,4},{3,5},{4,6},{5,7},{6,8},{7,9},{8,10},{9,11},{10,... | collective-permute-start | bytes 98312 | tf_op jit(solution)/shard_map/ppermute | solution.py:14
  449.7 8.5 %collective-permute-start.25 = (f32[32,256]{0,1:T(8,128)S(1)}, f32[32,256]{0,1:T(8,128)S(1)}, u32[]{:S(2)}, u32[]{:S(2)}) collective-permute-start(f32[32,256]{0,1:T(8,128)S(1)} %get-tuple-element.23), channel_id=1, source_target_pairs={{0,3},{1,4},{2,5},{3,6},{4,7},{5,8},{6,9},{7,10},{8,11},{9,12},{10... | collective-permute-start | bytes 98312 | tf_op jit(solution)/shard_map/ppermute | solution.py:14
  455.5 4.8 collective-permute-start.26
